TPU v7x, 256 devices: a whole 4x4x8 slice. The times are simulated.
256 devices in a mesh: pb: 16 (over x, z_hi), sa: 16 (over z_lo, y, core).
Axes of the slice: x: 4, y: 4, z: 8 (z_hi: 4, z_lo: 2; z = z_hi * 2 + z_lo), core: 2. Of those that a mesh axis runs over, the one named last changes fastest.
Arguments:
- question_states: bfloat16 [16, 16, 256, 768], P('pb', 'sa'), may hold values from -16 to 16
- question_ids: int32 [16, 16, 256], P('pb'), may hold values from 0 to 30521, as said below
- q_inner_weight: bfloat16 [768, 3072], P(None, 'sa'), may hold values from -0.21875 to 0.21875
- q_outer_weight: bfloat16 [3072, 768], P('sa'), may hold values from -0.109375 to 0.109375
- q_norm_gain: float32 [768], replicated, may hold values from 0.1 to 1.9
- sql_states: bfloat16 [16, 16, 256, 768], P('sa', 'pb'), may hold values from -16 to 16
- sql_ids: int32 [16, 16, 256], P('sa'), may hold values from 0 to 32099, as said below
- s_inner_weight: bfloat16 [768, 3072], P(None, 'pb'), may hold values from -0.21875 to 0.21875
- s_outer_weight: bfloat16 [3072, 768], P('pb'), may hold values from -0.109375 to 0.109375
- s_norm_gain: float32 [768], replicated, may hold values from 0.1 to 1.9
- positive_column: int32 [256], P('pb'), may hold values from 0 to 255, each once
Outputs:
- loss: float32 [], replicated
- q_inner_grad: float32 [768, 3072], P(None, 'sa')
- q_outer_grad: float32 [3072, 768], P('sa')
- q_gain_grad: float32 [768], replicated
- s_inner_grad: float32 [768, 3072], P(None, 'pb')
- s_outer_grad: float32 [3072, 768], P('pb')
- s_gain_grad: float32 [768], replicated
Inputs may be any that keep to these rules, and one draw needn't show every extreme that they name: `question_ids`: each sequence is a run of nonzero ids followed by padding zeros, the run 3 * 64 long or longer. `sql_ids`: each sequence is a run of nonzero ids followed by padding zeros, the run 3 * 64 long or longer.
All inputs are finite; a program needn't handle non-finite values.
Results may differ from a plain program's by a relative error of at most 0.0051.
Values may be sent and summed in bfloat16 or wider, within the bound.
A program may use at most 128 MiB of HBM per device.

v0:
```python
import math
import jax
import jax.numpy as jnp
from jax import lax
from jax.sharding import PartitionSpec as P

D = 768
HIGH = lax.Precision.HIGHEST


def apply_rms_norm(input_float, norm_gain_vector, root_mean_square):
    if root_mean_square:
        input_normalized = input_float * lax.rsqrt(
            jnp.mean(input_float * input_float, axis=-1, keepdims=True) + 1e-06
        )
    else:
        mean_removed = input_float - jnp.mean(input_float, axis=-1, keepdims=True)
        input_normalized = mean_removed * lax.rsqrt(
            jnp.mean(mean_removed * mean_removed, axis=-1, keepdims=True) + 1e-05
        )
    return (input_normalized, (input_normalized * norm_gain_vector).astype(jnp.bfloat16))


def gelu_value(v):
    return 0.5 * v * (1.0 + lax.erf(v / math.sqrt(2.0)))


def gelu_slope(v):
    return 0.5 * (1.0 + lax.erf(v / math.sqrt(2.0))) + v * jnp.exp(-0.5 * v * v) / math.sqrt(
        2.0 * math.pi
    )


def pool_weights(ids):
    mask = (ids > 0).astype(jnp.float32)
    return mask / jnp.sum(mask, axis=-1, keepdims=True)


def forward_block(states, ids, inner, norm_gain_vector, root_mean_square):
    count, length, width = states.shape
    input_float = states.astype(jnp.float32).reshape(count * length, width)
    input_normalized, normalized_rows = apply_rms_norm(
        input_float, norm_gain_vector, root_mean_square
    )
    pre = jnp.dot(normalized_rows, inner, preferred_element_type=jnp.float32)
    hidden = gelu_value(pre).reshape(count, length, -1)
    return jnp.einsum("nt,ntf->nf", pool_weights(ids), hidden, precision=HIGH)


def residual_pool(states, ids):
    return jnp.einsum("nt,ntd->nd", pool_weights(ids), states.astype(jnp.float32), precision=HIGH)


def backward_block(states, ids, inner, norm_gain_vector, root_mean_square, hidden_grad):
    count, length, width = states.shape
    input_float = states.astype(jnp.float32).reshape(count * length, width)
    input_normalized, normalized_rows = apply_rms_norm(
        input_float, norm_gain_vector, root_mean_square
    )
    pre = jnp.dot(normalized_rows, inner, preferred_element_type=jnp.float32)
    weights = pool_weights(ids)
    slope = gelu_slope(pre).reshape(count, length, -1)
    dpre = (
        (weights[:, :, None] * hidden_grad[:, None, :] * slope)
        .reshape(count * length, -1)
        .astype(jnp.bfloat16)
    )
    inner_layer_grad = lax.dot_general(
        normalized_rows, dpre, (((0,), (0,)), ((), ())), preferred_element_type=jnp.float32
    )
    normalized_grad = lax.dot_general(
        dpre, inner, (((1,), (1,)), ((), ())), preferred_element_type=jnp.float32
    )
    return (inner_layer_grad, jnp.sum(input_normalized * normalized_grad, axis=0))


def per_device(
    question_states,
    question_ids,
    q_inner_weight,
    q_outer_weight,
    q_norm_gain,
    sql_states,
    sql_ids,
    s_inner_weight,
    s_outer_weight,
    s_norm_gain,
    positive_column,
):
    scale = 1.0 / math.sqrt(D)
    q_table = question_ids[0]
    s_table = sql_ids[0]
    q_rows = q_table.shape[0]
    s_rows = s_table.shape[0]
    own_count = question_states.shape[1]
    q_place = lax.axis_index("sa")
    s_place = lax.axis_index("pb")

    def s_forward(piece):
        pooled = forward_block(piece[0], s_table, s_inner_weight, s_norm_gain, True)
        return pooled

    ids = q_table
    pooled = forward_block(
        lax.all_gather(question_states, "sa", axis=1, tiled=True)[0],
        ids,
        q_inner_weight,
        q_norm_gain,
        False,
    )
    s_pooled = s_forward(lax.all_gather(sql_states, "pb", axis=1, tiled=True))
    q_first = q_place * own_count
    s_first = s_place * own_count
    q_own = residual_pool(
        question_states[0], lax.dynamic_slice_in_dim(q_table, q_first, own_count, 0)
    )
    s_own = residual_pool(sql_states[0], lax.dynamic_slice_in_dim(s_table, s_first, own_count, 0))
    q_resid = lax.dynamic_update_slice_in_dim(
        jnp.zeros((q_rows, D), jnp.float32), q_own, q_first, 0
    )
    s_resid = lax.dynamic_update_slice_in_dim(
        jnp.zeros((s_rows, D), jnp.float32), s_own, s_first, 0
    )
    q_outer_f = q_outer_weight.astype(jnp.float32)
    s_outer_f = s_outer_weight.astype(jnp.float32)
    q_embed = lax.psum(jnp.dot(pooled, q_outer_f, precision=HIGH) + q_resid, "sa")
    s_embed = lax.psum(jnp.dot(s_pooled, s_outer_f, precision=HIGH) + s_resid, "pb")
    tile = scale * lax.dot_general(q_embed, s_embed, (((1,), (1,)), ((), ())), precision=HIGH)
    columns = q_place * s_rows + jnp.arange(s_rows, dtype=jnp.int32)
    match = (positive_column[:, None] == columns[None, :]).astype(jnp.float32)
    row_top = lax.pmax(jnp.max(tile, axis=1), "sa")
    row_total, row_pos = lax.psum(
        (jnp.sum(jnp.exp(tile - row_top[:, None]), axis=1), jnp.sum(match * tile, axis=1)), "sa"
    )
    col_top = lax.pmax(jnp.max(tile, axis=0), "pb")
    col_total, col_pos = lax.psum(
        (jnp.sum(jnp.exp(tile - col_top[None, :]), axis=0), jnp.sum(match * tile, axis=0)), "pb"
    )
    row_lse = row_top + jnp.log(row_total)
    col_lse = col_top + jnp.log(col_total)
    pairs = q_rows * lax.axis_size("pb")
    row_part = jnp.where(q_place == 0, jnp.sum(row_lse - row_pos), 0.0)
    col_part = jnp.where(s_place == 0, jnp.sum(col_lse - col_pos), 0.0)
    loss_part = (row_part + col_part) / (2.0 * pairs)
    dscore = 0.5 * (
        jnp.exp(tile - row_lse[:, None]) + jnp.exp(tile - col_lse[None, :]) - 2.0 * match
    )
    q_grad = lax.psum(scale * jnp.dot(dscore, s_embed, precision=HIGH), "sa")
    s_grad = lax.psum(
        scale * lax.dot_general(dscore, q_embed, (((0,), (0,)), ((), ())), precision=HIGH), "pb"
    )
    q_outer_part = lax.dot_general(pooled, q_grad, (((0,), (0,)), ((), ())), precision=HIGH)
    s_outer_part = lax.dot_general(s_pooled, s_grad, (((0,), (0,)), ((), ())), precision=HIGH)
    q_hidden_grad = lax.dot_general(q_grad, q_outer_f, (((1,), (1,)), ((), ())), precision=HIGH)
    s_hidden_grad = lax.dot_general(s_grad, s_outer_f, (((1,), (1,)), ((), ())), precision=HIGH)

    def s_backward(piece):
        inner_layer_grad, gain_grad = backward_block(
            piece[0], s_table, s_inner_weight, s_norm_gain, True, s_hidden_grad
        )
        return (inner_layer_grad, gain_grad)

    ids = q_table
    inner_layer_grad, gain_grad = backward_block(
        lax.all_gather(question_states, "sa", axis=1, tiled=True)[0],
        ids,
        q_inner_weight,
        q_norm_gain,
        False,
        q_hidden_grad,
    )
    s_inner_part, s_gain_part = s_backward(lax.all_gather(sql_states, "pb", axis=1, tiled=True))
    q_inner_grad, q_outer_grad = lax.psum((inner_layer_grad, q_outer_part), "pb")
    s_inner_grad, s_outer_grad = lax.psum((s_inner_part, s_outer_part), "sa")
    q_gain_grad, s_gain_grad, loss = lax.psum((gain_grad, s_gain_part, loss_part), ("pb", "sa"))
    return (loss, q_inner_grad, q_outer_grad, q_gain_grad, s_inner_grad, s_outer_grad, s_gain_grad)


def solution(mesh):
    placed = (
        P("pb", "sa", None, None),
        P("pb", None, None),
        P(None, "sa"),
        P("sa", None),
        P(),
        P("sa", "pb", None, None),
        P("sa", None, None),
        P(None, "pb"),
        P("pb", None),
        P(),
        P("pb"),
    )
    return jax.shard_map(
        per_device,
        mesh=mesh,
        in_specs=placed,
        out_specs=(P(), P(None, "sa"), P("sa", None), P(), P(None, "pb"), P("pb", None), P()),
        check_vma=False,
    )
```

profile of v0, /device:TPU:1, one launch (start us, length us, event | category | flops | bytes accessed | tf_op | source)
XLA Modules:
  0.0 849.9 jit_solution(1982385561405561287)
XLA Ops:
  15.7 43.4 %all-gather.3.cloned.1.call-done = bf16[1,16,256,768]{3,2,0,1:T(8,128)(2,1)} async-done(((bf16[1,1,256,768]{3,2,0,1:T(8,128)(2,1)}), bf16[1,16,256,768]{3,2,0,1:T(8,128)(2,1)}) %all-gather.3.cloned.1.call-update) | async-done | bytes 6291472 | tf_op jit(solution)/shard_map/all_gather | solution.py:105
  59.1 3.8 convert_reduce_fusion
  70.5 2.7 fusion.16
  74.9 56.9 %psum.105 = f32[16,768]{1,0:T(8,128)S(1)} all-reduce(f32[16,768]{1,0:T(8,128)S(1)} %add.105), channel_id=1, replica_groups=mesh['pb'=16,'sa'=16] {'sa'}, use_global_device_ids=true, to_apply=%region_4.0 | all-reduce | flops 12288 | bytes 98304 | tf_op jit(solution)/shard_map/psum | solution.py:126
  131.7 27.8 %all-gather.5.cloned.1.call-done = bf16[1,16,256,768]{3,2,0,1:T(8,128)(2,1)} async-done(((bf16[1,1,256,768]{3,2,0,1:T(8,128)(2,1)}), bf16[1,16,256,768]{3,2,0,1:T(8,128)(2,1)}) %all-gather.5.cloned.1.call-update) | async-done | bytes 6291472 | tf_op jit(solution)/shard_map/all_gather | solution.py:111
  159.5 4.2 multiply_reduce_fusion.2
  165.9 3.6 multiply_multiply_fusion.2
  169.6 2.7 fusion.13
  174.8 67.6 %psum.106 = f32[16,768]{1,0:T(8,128)} all-reduce(f32[16,768]{1,0:T(8,128)S(1)} %add.109), channel_id=1, replica_groups=mesh['pb'=16,'sa'=16] {'pb'}, use_global_device_ids=true, to_apply=%region_8.0 | all-reduce | flops 12288 | bytes 98304 | tf_op jit(solution)/shard_map/psum | solution.py:127
  243.6 41.3 %pmax.14 = f32[16]{0:T(128)S(1)} all-reduce(f32[16]{0:T(128)S(1)} %get-tuple-element.12), channel_id=1, replica_groups=mesh['pb'=16,'sa'=16] {'sa'}, use_global_device_ids=true, to_apply=%region_10.0 | all-reduce | flops 16 | bytes 128 | tf_op jit(solution)/shard_map/pmax | solution.py:131
  284.9 32.1 %pmax.15 = f32[16]{0:T(128)S(1)} all-reduce(f32[16]{0:T(128)S(1)} %get-tuple-element.11), channel_id=1, replica_groups=mesh['pb'=16,'sa'=16] {'pb'}, use_global_device_ids=true, to_apply=%region_17.0 | all-reduce | flops 16 | bytes 128 | tf_op jit(solution)/shard_map/pmax | solution.py:135
  318.3 34.1 %psum.107 = f32[16]{0:T(128)S(1)} all-reduce(f32[16]{0:T(128)S(1)} %get-tuple-element.10), channel_id=1, replica_groups=mesh['pb'=16,'sa'=16] {'sa'}, use_global_device_ids=true, to_apply=%region_12.0 | all-reduce | flops 16 | bytes 128 | tf_op jit(solution)/shard_map/psum | solution.py:132
  352.4 34.7 %psum.109 = f32[16]{0:T(128)S(1)} all-reduce(f32[16]{0:T(128)S(1)} %get-tuple-element.9), channel_id=1, replica_groups=mesh['pb'=16,'sa'=16] {'pb'}, use_global_device_ids=true, to_apply=%region_19.0 | all-reduce | flops 16 | bytes 128 | tf_op jit(solution)/shard_map/psum | solution.py:136
  390.5 56.9 %all-reduce.1 = (f32[16]{0:T(128)}, f32[16,768]{1,0:T(8,128)S(1)}) all-reduce(f32[16]{0:T(128)} %get-tuple-element.8, f32[16,768]{1,0:T(8,128)} %convolution_multiply_fusion.1), channel_id=1, replica_groups=mesh['pb'=16,'sa'=16] {'sa'}, use_global_device_ids=true, to_apply=%region_14.0 | all-reduce | flops 12304 | bytes 98432 | tf_op jit(solution)/shard_map/psum | solution.py:132
  451.4 4.4 copy.39
  455.8 63.2 %all-reduce.3 = (f32[16]{0:T(128)}, f32[16,768]{1,0:T(8,128)S(1)}) all-reduce(f32[16]{0:T(128)} %get-tuple-element.7, f32[16,768]{1,0:T(8,128)S(1)} %copy-done.27), channel_id=1, replica_groups=mesh['pb'=16,'sa'=16] {'pb'}, use_global_device_ids=true, to_apply=%region_21.0 | all-reduce | flops 12304 | bytes 98432 | tf_op jit(solution)/shard_map/psum | solution.py:136
  520.8 4.5 copy.42
  530.3 2.8 fusion.12
  534.6 5.0 fusion.66
  539.8 5.9 multiply_reduce_fusion
  548.2 4.8 multiply_reduce_fusion.1
  553.1 89.9 %all-reduce = (f32[]{:T(128)}, f32[768]{0:T(1024)}, f32[768]{0:T(1024)}) all-reduce(f32[]{:T(128)S(6)} %div.107, f32[768]{0:T(1024)S(1)} %multiply_reduce_fusion.1, f32[768]{0:T(1024)S(1)} %multiply_reduce_fusion), channel_id=1, replica_groups=mesh['pb'=16,'sa'=16] {'pb','sa'}, use_global_device_ids=true, to_apply=%region_23.24 | all-reduce | flops 1537 | bytes 12296 | tf_op jit(solution)/shard_map/psum | solution.py:175
  643.0 57.8 %all-reduce.10.cloned.1.call-done = (f32[768,192]{0,1:T(8,128)}, f32[192,768]{1,0:T(8,128)}) async-done(((f32[768,192]{0,1:T(8,128)}, f32[192,768]{1,0:T(8,128)}), (f32[768,192]{0,1:T(8,128)}, f32[192,768]{1,0:T(8,128)})) %all-reduce.10.cloned.1.call-update) | async-done | bytes 1179664 | tf_op jit(solution)/shard_map/psum | solution.py:173
  700.8 135.9 %all-reduce.8.cloned.1.call-done = (f32[768,192]{0,1:T(8,128)}, f32[192,768]{1,0:T(8,128)}) async-done(((f32[768,192]{0,1:T(8,128)}, f32[192,768]{1,0:T(8,128)}), (f32[768,192]{0,1:T(8,128)}, f32[192,768]{1,0:T(8,128)})) %all-reduce.8.cloned.1.call-update) | async-done | bytes 1179664 | tf_op jit(solution)/shard_map/psum | solution.py:174
  (135 shorter events, 46.8 us)
Async XLA Ops:
  7.2 158.7 %copy-start = (bf16[768,192]{0,1:T(8,128)(2,1)S(1)}, bf16[768,192]{0,1:T(8,128)(2,1)}, u32[]{:S(2)}) copy-start(bf16[768,192]{0,1:T(8,128)(2,1)} %param.18) | copy-start | bytes 884740
  7.2 51.9 %all-gather.3.cloned.1.call-start = ((), (), s32[]{:S(2)}) async-start(), calls=%async_computation | async-start | bytes 6684672 | tf_op jit(solution)/shard_map/all_gather | solution.py:105
  7.9 151.6 %all-gather.5.cloned.1.call-start = ((), (), s32[]{:S(2)}) async-start(), calls=%async_computation.1 | async-start | bytes 6684672 | tf_op jit(solution)/shard_map/all_gather | solution.py:111
  8.7 692.1 %all-reduce.10.cloned.1.call-start = ((), (), s32[]{:S(2)}) async-start(), calls=%async_computation.3 | async-start | bytes 2359296 | tf_op jit(solution)/shard_map/psum | solution.py:173
  59.1 4.6 copy-start.1
  131.7 32.7 %copy-start.29 = (f32[768]{0:T(1024)S(1)}, f32[768]{0:T(1024)}, u32[]{:S(2)}) copy-start(f32[768]{0:T(1024)} %param.20) | copy-start | bytes 9220
  159.5 4.9 copy-start.4
  165.9 3.7 copy-start.3
  352.4 38.1 %copy-start.34 = (f32[16]{0:T(128)}, f32[16]{0:T(128)S(1)}, u32[]{:S(2)}) copy-start(f32[16]{0:T(128)S(1)} %log_add_fusion.1) | copy-start | bytes 196
  451.4 4.4 copy-start.27
  520.7 4.6 copy-start.6
  520.7 4.6 copy-start.19
  520.8 7.1 slice-start
  530.2 306.5 %all-reduce.8.cloned.1.call-start = ((), (), s32[]{:S(2)}) async-start(), calls=%async_computation.2 | async-start | bytes 2359296 | tf_op jit(solution)/shard_map/psum | solution.py:174
  534.6 5.1 copy-start.26
  539.7 6.0 copy-start.30
  539.7 6.0 copy-start.35
  539.7 7.2 copy-start.31
  539.7 7.2 copy-start.33
  539.7 8.5 copy-start.10
  539.7 8.5 copy-start.16
  539.7 8.5 copy-start.22
  539.7 8.5 copy-start.24
  836.7 5.8 copy-start.14
  (18 other events, 41.1 us)
Sparse Core Ops, SparseCore 0:
  9.9 49.1 all-gather.2
  61.5 97.9 all-gather.4
  530.3 170.4 all-reduce.9
  703.9 132.7 all-reduce.7
where the time goes:
time: 851 us; the launch traced here: 850 us
  blocking collectives  477 us (56%)
  waiting for transfers between devices  266 us (31%)
  matrix products  43.3 us (5%)
  other arithmetic  26 us (3%)
  local copies, waits for them, and re-layouts  20.5 us (2%)
  between operations  17 us (2%)
    psum x1, waiting for transfers between devices, per_device(): s_inner_grad, s_outer_grad = lax.psum((s_inner_part, s_outer_part), 'sa')  136 us
    psum x2, blocking collectives, per_device(): lax.psum((jnp.sum(jnp.exp(tile - col_top[None, :]), axis=0), jnp.sum(matc...  97.9 us
    psum x2, blocking collectives, per_device(): lax.psum((jnp.sum(jnp.exp(tile - row_top[:, None]), axis=1), jnp.sum(matc...  91 us
    psum x1, blocking collectives, per_device(): lax.psum((gain_grad, s_gain_part, loss_part), ('pb', 'sa'))  89.9 us
    psum x1, blocking collectives, per_device(): lax.psum(jnp.dot(s_pooled, s_outer_f, precision=HIGH) + s_resid, 'pb')  67.6 us
    psum x1, waiting for transfers between devices, per_device(): lax.psum((inner_layer_grad, q_outer_part), 'pb')  57.8 us
    psum x1, blocking collectives, per_device(): lax.psum(jnp.dot(pooled, q_outer_f, precision=HIGH) + q_resid, 'sa')  56.9 us
    all_gather x1, waiting for transfers between devices, per_device(): lax.all_gather(question_states, 'sa', axis=1, tiled=True)[0]  43.4 us
  transfers between devices with their start and end apart: 4, of which 4 were waited for; matrix products, arithmetic and copies ran while one was open for 5% of the time, Pallas kernels for 0%

commit v1 on v0

--- a/solution.py
+++ b/solution.py
@@ -1,11 +1,26 @@
+import functools
 import math
 import jax
 import jax.numpy as jnp
 from jax import lax
 from jax.sharding import PartitionSpec as P
+from jax.lax import all_to_all, axis_size
 
 D = 768
 HIGH = lax.Precision.HIGHEST
+
+
+def put_leaf(body, net_axis, dim_k):
+    local_part = jnp.concatenate(
+        all_to_all(
+            jnp.stack([body] * axis_size(net_axis)), split_axis=0, concat_axis=0, axis_name=net_axis
+        ),
+        axis=dim_k,
+    )
+    return local_part
+
+
+keep_up_the_numbers = functools.partial(put_leaf, net_axis="pb", dim_k=1)
 
 
 def apply_rms_norm(input_float, norm_gain_vector, root_mean_square):
@@ -108,7 +123,7 @@
         q_norm_gain,
         False,
     )
-    s_pooled = s_forward(lax.all_gather(sql_states, "pb", axis=1, tiled=True))
+    s_pooled = s_forward(keep_up_the_numbers(sql_states))
     q_first = q_place * own_count
     s_first = s_place * own_count
     q_own = residual_pool(

time: 851 us -> 1050 us (1.23)
  waiting for transfers between devices: 266 us -> 433 us
  starting transfers between devices: 0.16 us -> 12.2 us
    all_gather x1, waiting for transfers between devices: 27.8 us -> 196 us  [per_device(): lax.all_gather(sql_states, 'pb', axis=1, tiled=True)]
    all_to_all x0 -> x1, starting transfers between devices: none -> 11.8 us  [put_leaf(): all_to_all(jnp.stack([body] * axis_size(net_axis)), split_axis=0, concat_...]
  transfers between devices with their start and end apart: 4 -> 5, of which waited for: 4 -> 4; matrix products, arithmetic and copies ran while one was open for 5% -> 4% of each run, Pallas kernels for 0% -> 0%
where the time goes in v1:
time: 1050 us; the launch traced here: 1040 us
  blocking collectives  475 us (45%)
  waiting for transfers between devices  433 us (41%)
  matrix products  47.7 us (5%)
  other arithmetic  34 us (3%)
  local copies, waits for them, and re-layouts  24.4 us (2%)
  between operations  17.1 us (2%)
  starting transfers between devices  12.2 us (1%)
    all_gather x1, waiting for transfers between devices, per_device(): lax.all_gather(sql_states, 'pb', axis=1, tiled=True)  196 us
    psum x1, waiting for transfers between devices, per_device(): s_inner_grad, s_outer_grad = lax.psum((s_inner_part, s_outer_part), 'sa')  136 us
    psum x2, blocking collectives, per_device(): lax.psum((jnp.sum(jnp.exp(tile - col_top[None, :]), axis=0), jnp.sum(matc...  99 us
    psum x1, blocking collectives, per_device(): lax.psum((gain_grad, s_gain_part, loss_part), ('pb', 'sa'))  90.2 us
    psum x2, blocking collectives, per_device(): lax.psum((jnp.sum(jnp.exp(tile - row_top[:, None]), axis=1), jnp.sum(matc...  84.1 us
    psum x1, blocking collectives, per_device(): lax.psum(jnp.dot(s_pooled, s_outer_f, precision=HIGH) + s_resid, 'pb')  68.8 us
    psum x1, blocking collectives, per_device(): lax.psum(jnp.dot(pooled, q_outer_f, precision=HIGH) + q_resid, 'sa')  63.3 us
    psum x1, waiting for transfers between devices, per_device(): lax.psum((inner_layer_grad, q_outer_part), 'pb')  55.8 us
  transfers between devices with their start and end apart: 5, of which 4 were waited for; matrix products, arithmetic and copies ran while one was open for 4% of the time, Pallas kernels for 0%

profile of v1, /device:TPU:1, one launch (start us, length us, event | category | flops | bytes accessed | tf_op | source)
XLA Modules:
  0.0 1044.0 jit_solution(594147175180576336)
XLA Ops:
  8.7 4.2 stack.2
  12.9 11.8 %all-to-all-start = ((bf16[16,1,1,256,768]{4,3,2,1,0:T(8,128)(2,1)}), bf16[16,1,1,256,768]{4,3,2,1,0:T(8,128)(2,1)}, u32[]{:S(2)}, u32[]{:S(2)}) async-start(bf16[16,1,1,256,768]{4,3,2,1,0:T(8,128)(2,1)} %stack.2), calls=%async_computation | async-start | bytes 12582912 | tf_op jit(solution)/shard_map/all_to_all | solution.py:15
  28.9 195.6 %all-gather.5.cloned.1.call-done = bf16[1,16,256,768]{3,2,0,1:T(8,128)(2,1)} async-done(((bf16[1,1,256,768]{3,2,0,1:T(8,128)(2,1)}), bf16[1,16,256,768]{3,2,0,1:T(8,128)(2,1)}) %all-gather.5.cloned.1.call-update) | async-done | bytes 6291472 | tf_op jit(solution)/shard_map/all_gather | solution.py:187
  224.5 4.1 multiply_reduce_fusion.1
  228.6 44.5 %all-gather.3.cloned.1.call-done = bf16[1,16,256,768]{3,2,0,1:T(8,128)(2,1)} async-done(((bf16[1,1,256,768]{3,2,0,1:T(8,128)(2,1)}), bf16[1,16,256,768]{3,2,0,1:T(8,128)(2,1)}) %all-gather.3.cloned.1.call-update) | async-done | bytes 6291472 | tf_op jit(solution)/shard_map/all_gather | solution.py:120
  273.1 3.8 convert_reduce_fusion
  279.7 4.1 multiply_reduce_fusion.3
  283.9 8.6 multiply_convert_fusion
  298.2 68.8 %psum.106 = f32[16,768]{1,0:T(8,128)S(1)} all-reduce(f32[16,768]{1,0:T(8,128)S(1)} %add.119), channel_id=1, replica_groups=mesh['pb'=16,'sa'=16] {'pb'}, use_global_device_ids=true, to_apply=%region_8.0 | all-reduce | flops 12288 | bytes 98304 | tf_op jit(solution)/shard_map/psum | solution.py:142
  367.1 4.6 multiply_convert_fusion.1
  379.9 63.3 %psum.105 = f32[16,768]{1,0:T(8,128)} all-reduce(f32[16,768]{1,0:T(8,128)S(1)} %add.115), channel_id=1, replica_groups=mesh['pb'=16,'sa'=16] {'sa'}, use_global_device_ids=true, to_apply=%region_4.0 | all-reduce | flops 12288 | bytes 98304 | tf_op jit(solution)/shard_map/psum | solution.py:141
  444.3 32.1 %pmax.15 = f32[16]{0:T(128)S(1)} all-reduce(f32[16]{0:T(128)S(1)} %get-tuple-element.11), channel_id=1, replica_groups=mesh['pb'=16,'sa'=16] {'pb'}, use_global_device_ids=true, to_apply=%region_17.0 | all-reduce | flops 16 | bytes 128 | tf_op jit(solution)/shard_map/pmax | solution.py:150
  476.5 37.8 %pmax.14 = f32[16]{0:T(128)S(1)} all-reduce(f32[16]{0:T(128)S(1)} %get-tuple-element.12), channel_id=1, replica_groups=mesh['pb'=16,'sa'=16] {'sa'}, use_global_device_ids=true, to_apply=%region_10.0 | all-reduce | flops 16 | bytes 128 | tf_op jit(solution)/shard_map/pmax | solution.py:146
  515.7 34.7 %psum.109 = f32[16]{0:T(128)S(1)} all-reduce(f32[16]{0:T(128)S(1)} %get-tuple-element.9), channel_id=1, replica_groups=mesh['pb'=16,'sa'=16] {'pb'}, use_global_device_ids=true, to_apply=%region_19.0 | all-reduce | flops 16 | bytes 128 | tf_op jit(solution)/shard_map/psum | solution.py:151
  550.4 34.4 %psum.107 = f32[16]{0:T(128)S(1)} all-reduce(f32[16]{0:T(128)S(1)} %get-tuple-element.10), channel_id=1, replica_groups=mesh['pb'=16,'sa'=16] {'sa'}, use_global_device_ids=true, to_apply=%region_12.0 | all-reduce | flops 16 | bytes 128 | tf_op jit(solution)/shard_map/psum | solution.py:147
  588.1 49.7 %all-reduce.1 = (f32[16]{0:T(128)}, f32[16,768]{1,0:T(8,128)S(1)}) all-reduce(f32[16]{0:T(128)} %get-tuple-element.8, f32[16,768]{1,0:T(8,128)} %convolution_multiply_fusion.1), channel_id=1, replica_groups=mesh['pb'=16,'sa'=16] {'sa'}, use_global_device_ids=true, to_apply=%region_14.0 | all-reduce | flops 12304 | bytes 98432 | tf_op jit(solution)/shard_map/psum | solution.py:147
  642.0 64.2 %all-reduce.3 = (f32[16]{0:T(128)}, f32[16,768]{1,0:T(8,128)}) all-reduce(f32[16]{0:T(128)} %get-tuple-element.7, f32[16,768]{1,0:T(8,128)} %convolution_multiply_fusion), channel_id=1, replica_groups=mesh['pb'=16,'sa'=16] {'pb'}, use_global_device_ids=true, to_apply=%region_21.0 | all-reduce | flops 12304 | bytes 98432 | tf_op jit(solution)/shard_map/psum | solution.py:151
  719.5 4.4 copy.42
  724.2 7.7 fusion.14
  735.5 5.9 multiply_reduce_fusion
  743.9 4.9 multiply_reduce_fusion.2
  748.8 90.2 %all-reduce = (f32[]{:T(128)}, f32[768]{0:T(1024)}, f32[768]{0:T(1024)}) all-reduce(f32[]{:T(128)S(6)} %div.111, f32[768]{0:T(1024)S(1)} %multiply_reduce_fusion.2, f32[768]{0:T(1024)S(1)} %multiply_reduce_fusion), channel_id=1, replica_groups=mesh['pb'=16,'sa'=16] {'pb','sa'}, use_global_device_ids=true, to_apply=%region_23.24 | all-reduce | flops 1537 | bytes 12296 | tf_op jit(solution)/shard_map/psum | solution.py:190
  839.0 55.8 %all-reduce.10.cloned.1.call-done = (f32[768,192]{0,1:T(8,128)}, f32[192,768]{1,0:T(8,128)}) async-done(((f32[768,192]{0,1:T(8,128)}, f32[192,768]{1,0:T(8,128)}), (f32[768,192]{0,1:T(8,128)}, f32[192,768]{1,0:T(8,128)})) %all-reduce.10.cloned.1.call-update) | async-done | bytes 1179664 | tf_op jit(solution)/shard_map/psum | solution.py:188
  894.8 136.0 %all-reduce.8.cloned.1.call-done = (f32[768,192]{0,1:T(8,128)}, f32[192,768]{1,0:T(8,128)}) async-done(((f32[768,192]{0,1:T(8,128)}, f32[192,768]{1,0:T(8,128)}), (f32[768,192]{0,1:T(8,128)}, f32[192,768]{1,0:T(8,128)})) %all-reduce.8.cloned.1.call-update) | async-done | bytes 1179664 | tf_op jit(solution)/shard_map/psum | solution.py:189
  (138 shorter events, 55.6 us)
Async XLA Ops:
  7.2 285.3 %copy-start = (bf16[768,192]{0,1:T(8,128)(2,1)S(1)}, bf16[768,192]{0,1:T(8,128)(2,1)}, u32[]{:S(2)}) copy-start(bf16[768,192]{0,1:T(8,128)(2,1)} %param.18) | copy-start | bytes 884740
  7.2 217.3 %all-gather.5.cloned.1.call-start = ((), (), s32[]{:S(2)}) async-start(), calls=%async_computation.2 | async-start | bytes 6684672 | tf_op jit(solution)/shard_map/all_gather | solution.py:187
  7.9 265.2 %all-gather.3.cloned.1.call-start = ((), (), s32[]{:S(2)}) async-start(), calls=%async_computation.1 | async-start | bytes 6684672 | tf_op jit(solution)/shard_map/all_gather | solution.py:120
  12.9 11.8 %copy-start.20 = (s32[1,16,256]{2,1,0:T(8,128)S(1)}, s32[1,16,256]{2,1,0:T(8,128)}, u32[]{:S(2)}) copy-start(s32[1,16,256]{2,1,0:T(8,128)} %param.17) | copy-start | bytes 49156
  12.9 11.8 %copy-start.21 = (s32[1,16,256]{2,1,0:T(8,128)S(1)}, s32[1,16,256]{2,1,0:T(8,128)}, u32[]{:S(2)}) copy-start(s32[1,16,256]{2,1,0:T(8,128)} %param.12) | copy-start | bytes 49156
  12.9 266.8 %all-to-all-start = ((bf16[16,1,1,256,768]{4,3,2,1,0:T(8,128)(2,1)}), bf16[16,1,1,256,768]{4,3,2,1,0:T(8,128)(2,1)}, u32[]{:S(2)}, u32[]{:S(2)}) async-start(bf16[16,1,1,256,768]{4,3,2,1,0:T(8,128)(2,1)} %stack.2), calls=%async_computation | async-start | bytes 12582912 | tf_op jit(solution)/shard_map/all_to_all | solution.py:15
  24.7 870.2 %all-reduce.10.cloned.1.call-start = ((), (), s32[]{:S(2)}) async-start(), calls=%async_computation.4 | async-start | bytes 2359296 | tf_op jit(solution)/shard_map/psum | solution.py:188
  228.6 55.2 %copy-start.18 = (f32[2,2,8,128]{3,1,2,0:T(2,128)}, f32[2,2,8,128]{3,1,2,0:T(2,128)S(1)}, u32[]{:S(2)}) copy-start(f32[2,2,8,128]{3,1,2,0:T(2,128)S(1)} %copy.43) | copy-start | bytes 49156
  277.0 90.1 %copy-start.14 = (f32[2,2,8,128]{3,1,2,0:T(2,128)}, f32[2,2,8,128]{3,1,2,0:T(2,128)S(1)}, u32[]{:S(2)}) copy-start(f32[2,2,8,128]{3,1,2,0:T(2,128)S(1)} %copy.34) | copy-start | bytes 49156
  279.7 87.4 %copy-start.16 = (f32[2,2,8,128]{3,1,2,0:T(2,128)}, f32[2,2,8,128]{3,1,2,0:T(2,128)S(1)}, u32[]{:S(2)}) copy-start(f32[2,2,8,128]{3,1,2,0:T(2,128)S(1)} %copy.35) | copy-start | bytes 49156
  294.9 72.1 %copy-start.23 = (f32[768]{0:T(1024)S(1)}, f32[768]{0:T(1024)}, u32[]{:S(2)}) copy-start(f32[768]{0:T(1024)} %param.15) | copy-start | bytes 9220
  550.4 37.7 %copy-start.27 = (f32[16]{0:T(128)}, f32[16]{0:T(128)S(1)}, u32[]{:S(2)}) copy-start(f32[16]{0:T(128)S(1)} %log_add_fusion) | copy-start | bytes 196
  723.9 9.3 slice-start.2
  723.9 306.9 %all-reduce.8.cloned.1.call-start = ((), (), s32[]{:S(2)}) async-start(), calls=%async_computation.3 | async-start | bytes 2359296 | tf_op jit(solution)/shard_map/psum | solution.py:189
  724.2 8.9 slice-start.3
  735.4 6.0 copy-start.25
  735.4 6.0 copy-start.30
  735.4 7.2 copy-start.26
  735.4 7.2 copy-start.28
  735.4 8.5 copy-start.6
  735.4 8.5 copy-start.11
  735.4 8.5 copy-start.15
  735.4 8.5 copy-start.17
  1030.8 5.8 copy-start.9
  (17 other events, 51.9 us)
Sparse Core Ops, SparseCore 0:
  10.5 213.9 all-gather.4
  226.3 46.7 all-gather.2
  724.0 170.7 all-reduce.9
  897.9 132.8 all-reduce.7
